TPU v7x, 256 devices: a whole 4x4x8 slice. The times are simulated.
256 devices in a mesh: fibre: 64 (over y_lo, x, z), seg: 4 (over y_hi, core).
Axes of the slice: x: 4, y: 4 (y_hi: 2, y_lo: 2; y = y_hi * 2 + y_lo), z: 8, core: 2. Of those that a mesh axis runs over, the one named last changes fastest.
Arguments:
- strain: float32 [6144, 2048], P(('fibre', 'seg')), may hold values from -500 to 500
- fir_taps: float32 [64], replicated, may hold values from -0.75 to 0.75
- space_taps: float32 [31], replicated, may hold values from -1.2 to 1.2
- sources: int32 [3, 4], replicated, may hold values from 0 to 6143, as said below
Outputs:
- correlations: float32 [3, 4, 6144, 256], P(None, None, ('fibre', 'seg'))
Inputs may be any that keep to these rules, and one draw needn't show every extreme that they name: `sources`: virtual-source channel indices; repeats are allowed.
All inputs are finite; a program needn't handle non-finite values.
Results may differ from a plain program's by a relative error of at most 0.0028.
Values may be sent and summed in bfloat16 or wider, within the bound.
A program may use at most 64 MiB of HBM per device.

v0:
```python
import functools

import jax
import jax.numpy as jnp
from jax import lax
from jax.experimental import pallas as pl
from jax.experimental.pallas import tpu as pltpu
from jax.sharding import PartitionSpec as P

MESH = pl.DeviceIdType.MESH
F32 = jnp.float32
BF16 = jnp.bfloat16

CH = 24
BLOCKS = 16
SAMPLES = BLOCKS * 128
TAPS = 64
SPACE = 31
HALF = 15
RUN = 64
SRCS = 12
SROWS = 16
FINE = 16
COARSE = 8
PIECES = 32


def source_row(i):
    return i if i < 6 else i + 2


def dot(a, b, contract=((1,), (0,))):
    return lax.dot_general(a, b, (contract, ((), ())), preferred_element_type=F32)


def split(x):
    high = x.astype(BF16)
    return high, (x - high.astype(F32)).astype(BF16)


def iota(shape, dim):
    return lax.broadcasted_iota(jnp.int32, shape, dim)


def three_pass_weights(w, part):
    high, low = split(w)
    picked = jnp.where(part == 1, low.astype(F32), high.astype(F32))
    return picked.astype(BF16)


def source_weights(src_ref, space_ref, first):
    shape = (SROWS, 128)
    row, lane = iota(shape, 0), iota(shape, 1)
    chosen = jnp.full(shape, -(1 << 20), jnp.int32)
    for i in range(SRCS):
        chosen = jnp.where(row == source_row(i), src_ref[i // 4, i % 4], chosen)
    part, r = lane // 32, lane % 32
    tap = jnp.where(r < CH, first + r - chosen + HALF, -1)
    w = jnp.zeros(shape, F32)
    for k in range(SPACE):
        w = jnp.where(tap == k, space_ref[k], w)
    return three_pass_weights(w, part)[:, :96]


def own_weights(space_ref, first, channels):
    shape = (CH, 256)
    row, lane = iota(shape, 0), iota(shape, 1)
    part, r = lane // 64, lane % 64
    rel = jnp.where(r < 32, r, jnp.where(r < 48, r - 48, r - 24))
    inside = (first + rel >= 0) & (first + rel < channels) & ((r < CH) | (r >= 32))
    tap = jnp.where(inside, rel - row + HALF, -1)
    w = jnp.zeros(shape, F32)
    for k in range(SPACE):
        w = jnp.where(tap == k, space_ref[k], w)
    return three_pass_weights(w, part)[:, :192]


def fir_weights(fir_ref):
    lane = iota((8, 128), 1)
    v = jnp.zeros((8, 128), F32)
    for k in range(TAPS):
        v = jnp.where(lane == k, fir_ref[k], v)
    turned = pltpu.roll(
        jnp.broadcast_to(v[0:1], (128, 128)), 0, 1, stride=1, stride_axis=0
    )
    u, t = iota((128, 128), 0), iota((128, 128), 1)
    now = jnp.where(t >= u, turned, 0.0)
    later = jnp.where(t < u, turned, 0.0)
    high, low = split(jnp.concatenate([now, later], axis=1))
    return jnp.concatenate([high, high, low], axis=0)


def window_weights():
    u, t = iota((128, 128), 0), iota((128, 128), 1)
    here = jnp.abs(u - t) <= RUN
    after = u - t >= RUN
    before = t - u >= RUN
    one = jnp.concatenate(
        [jnp.where(m, 1.0, 0.0).astype(F32) for m in (here, after, before)], axis=1
    ).astype(BF16)
    return jnp.concatenate([one, one], axis=0)


def normalized(x, rows, fir_w, win_w):
    high, low = split(x)
    g = dot(jnp.concatenate([high, low, high], axis=1), fir_w)
    zero = jnp.zeros((rows, 128), F32)
    smooth = g[:, :128] + jnp.concatenate([zero, g[:-rows, 128:]], axis=0)
    high, low = split(jnp.abs(smooth))
    g = dot(jnp.concatenate([high, low], axis=1), win_w)
    total = (
        g[:, :128]
        + jnp.concatenate([zero, g[:-rows, 128:256]], axis=0)
        + jnp.concatenate([g[rows:, 256:], zero], axis=0)
    )
    t = iota((rows, 128), 1)
    first = (jnp.minimum(t, RUN) + (RUN + 1)).astype(F32)
    last = (jnp.minimum(127 - t, RUN) + (RUN + 1)).astype(F32)
    level = jnp.concatenate(
        [
            total[:rows] / first,
            total[rows:-rows] * (1.0 / (2 * RUN + 1)),
            total[-rows:] / last,
        ],
        axis=0,
    )
    return smooth / (level + 1e-5)


def kernel(
    nf, ns, nz,
    fir_ref, space_ref, src_ref, strain_ref, out_ref,
    x_ref, halo_ref, send1, recv1, send2, recv2, gathered,
    fir_w, win_w, own_w, n_ref, s_ref, q_ref, a_ref,
    load_sem, sems, halo_sems,
):
    nq = (nf // nz) * ns
    own = PIECES // nq
    f, g = lax.axis_index("fibre"), lax.axis_index("seg")
    plane = lax.div(f, nz) * ns + g
    z = lax.rem(f, nz)
    line = f * ns + g
    count = nf * ns

    def in_plane(step):
        other = lax.rem(plane + step, nq)
        return (lax.div(other, ns) * nz + z, lax.rem(other, ns)), other

    def along_z(step):
        return (lax.div(f, nz) * nz + lax.rem(z + step, nz), g)

    def on_line(step):
        other = lax.rem(line + step + count, count)
        return (lax.div(other, ns), lax.rem(other, ns))

    load = pltpu.make_async_copy(strain_ref, x_ref, load_sem)
    load.start()
    gathered[...] = jnp.zeros_like(gathered)
    barrier = pltpu.get_barrier_semaphore()

    @pl.loop(1, nq)
    def _(step):
        pl.semaphore_signal(barrier, inc=1, device_id=in_plane(step)[0], device_id_type=MESH)

    @pl.loop(1, nz)
    def _(step):
        pl.semaphore_signal(barrier, inc=1, device_id=along_z(step), device_id_type=MESH)

    for step in (-1, 1):
        pl.semaphore_signal(barrier, inc=1, device_id=on_line(step), device_id_type=MESH)

    first_channel = line * CH
    source_w = source_weights(src_ref, space_ref, first_channel)
    load.wait()
    pad = jnp.zeros((8, SAMPLES), F32)
    high, low = split(jnp.concatenate([x_ref[...], pad], axis=0))
    part = dot(source_w, jnp.concatenate([high, high, low], axis=0))
    for b in range(BLOCKS):
        for h in range(2):
            send1[2 * b + h] = part[8 * h : 8 * h + 8, 128 * b : 128 * b + 128]

    pl.semaphore_wait(barrier, nq - 1 + nz - 1 + 2)

    def plane_copy(step):
        device, other = in_plane(step)
        return pltpu.make_async_remote_copy(
            src_ref=send1.at[pl.ds(other * own, own), pl.ds(0, 6)],
            dst_ref=recv1.at[step, :, pl.ds(0, 6)],
            send_sem=sems.at[0], recv_sem=sems.at[1],
            device_id=device, device_id_type=MESH,
        )

    def z_copy(step):
        return pltpu.make_async_remote_copy(
            src_ref=send2.at[:, pl.ds(0, 6)],
            dst_ref=recv2.at[step, :, pl.ds(0, 6)],
            send_sem=sems.at[2], recv_sem=sems.at[3],
            device_id=along_z(step), device_id_type=MESH,
        )

    def gather_copy(step):
        mine = gathered.at[pl.ds(plane * own, own), pl.ds(0, 6)]
        return pltpu.make_async_remote_copy(
            src_ref=mine, dst_ref=mine,
            send_sem=sems.at[4], recv_sem=sems.at[5],
            device_id=in_plane(step)[0], device_id_type=MESH,
        )

    def bulk(ref, first, device):
        return pltpu.make_async_remote_copy(
            src_ref=ref, dst_ref=ref,
            send_sem=sems.at[first], recv_sem=sems.at[first + 1],
            device_id=device, device_id_type=MESH,
        )

    up = pltpu.make_async_remote_copy(
        src_ref=x_ref.at[pl.ds(CH - 16, 16)], dst_ref=halo_ref.at[0],
        send_sem=halo_sems.at[0], recv_sem=halo_sems.at[1],
        device_id=on_line(1), device_id_type=MESH,
    )
    down = pltpu.make_async_remote_copy(
        src_ref=x_ref.at[pl.ds(0, 16)], dst_ref=halo_ref.at[1],
        send_sem=halo_sems.at[2], recv_sem=halo_sems.at[3],
        device_id=on_line(-1), device_id_type=MESH,
    )

    @pl.loop(1, nq)
    def _(step):
        plane_copy(step).start()

    fir_w[...] = fir_weights(fir_ref)
    win_w[...] = window_weights()
    own_w[...] = own_weights(space_ref, first_channel, count * CH)
    a_ref[SRCS * FINE :, :] = jnp.zeros((256 - SRCS * FINE, a_ref.shape[1]), BF16)

    all_plane = bulk(recv1.at[pl.ds(1, nq - 1), :, pl.ds(0, 6)], 0, in_plane(1)[0])
    all_z = bulk(recv2.at[pl.ds(1, nz - 1), :, pl.ds(0, 6)], 2, along_z(1))
    all_gather = bulk(gathered.at[pl.ds(0, (nq - 1) * own), pl.ds(0, 6)], 4, in_plane(1)[0])

    all_plane.wait_recv()
    total = send1[pl.ds(plane * own, own), 0:6, :]
    for step in range(1, nq):
        total = total + recv1[step, :, 0:6, :]
    send2[:, 0:6, :] = total

    @pl.loop(1, nz)
    def _(step):
        z_copy(step).start()

    up.start()
    down.start()

    all_z.wait_recv()
    for step in range(1, nz):
        total = total + recv2[step, :, 0:6, :]
    gathered[pl.ds(plane * own, own), 0:6, :] = total

    @pl.loop(1, nq)
    def _(step):
        gather_copy(step).start()

    up.wait_recv()
    down.wait_recv()
    high, low = split(jnp.concatenate([x_ref[...], pad, halo_ref[0], halo_ref[1]], axis=0))
    spatial = dot(own_w[...], jnp.concatenate([high, high, low], axis=0))
    blocks = jnp.concatenate(
        [spatial[:, 128 * b : 128 * b + 128] for b in range(BLOCKS)], axis=0
    )
    n_ref[...] = normalized(blocks, CH, fir_w[...], win_w[...])
    lane = iota((CH, 128), 1)
    none = [jnp.zeros((CH, 128), F32)] * COARSE

    def turned_blocks(b):
        if not 0 <= b < BLOCKS:
            return none
        block = n_ref[b * CH : b * CH + CH]
        return [block] + [pltpu.roll(block, 128 - 16 * k, 1) for k in range(1, COARSE)]

    here = none
    for b in range(-1, BLOCKS + 1):
        following = turned_blocks(b + 1)
        shifted = [
            jnp.where(lane < 128 - 16 * k, here[k], following[k]) for k in range(COARSE)
        ]
        q_ref[:, (b + 1) * 128 : (b + 2) * 128] = jnp.concatenate(shifted, axis=0).astype(BF16)
        here = following

    all_gather.wait_recv()
    records = gathered[...].reshape(BLOCKS * SROWS, 128)
    s_ref[...] = normalized(records, SROWS, fir_w[...], win_w[...])
    shift, lane = iota((FINE, 128), 0), iota((FINE, 128), 1)
    for i in range(SRCS):
        before = jnp.zeros((FINE, 128), F32)
        for b in range(BLOCKS + 1):
            if b < BLOCKS:
                row = b * SROWS + source_row(i)
                wide = jnp.broadcast_to(s_ref[row : row + 1, :], (FINE, 128))
                here = pltpu.roll(wide, 0, 1, stride=1, stride_axis=0)
            else:
                here = jnp.zeros((FINE, 128), F32)
            a_ref[FINE * i : FINE * i + FINE, 128 * b : 128 * b + 128] = jnp.where(
                lane >= shift, here, before
            ).astype(BF16)
            before = here

    width = (BLOCKS + 1) * 128
    lane = iota((CH, 128), 1)
    factor = float(SAMPLES) ** -0.5
    for half in range(2):
        d = dot(q_ref[:, 128 * half : 128 * half + width], a_ref[...], ((1,), (1,)))
        for tile in range(2):
            v = [
                d[CH * k : CH * k + CH, 128 * tile : 128 * tile + 128] * factor
                for k in range(COARSE)
            ]
            for bit in (1, 2, 4):
                low_part = (lax.div(lane, 16) & bit) == 0
                for k in range(COARSE):
                    if k & bit:
                        continue
                    a, b = v[k], v[k | bit]
                    v[k] = jnp.where(low_part, a, pltpu.roll(b, 16 * bit, 1))
                    v[k | bit] = jnp.where(low_part, pltpu.roll(a, 128 - 16 * bit, 1), b)
            for k in range(COARSE):
                if COARSE * tile + k < SRCS:
                    out_ref[COARSE * tile + k, :, 128 * half : 128 * half + 128] = v[k]

    all_plane.wait_send()
    all_z.wait_send()
    all_gather.wait_send()
    up.wait_send()
    down.wait_send()


def local(nf, ns, nz, strain, fir_taps, space_taps, sources):
    nq = (nf // nz) * ns
    own = PIECES // nq
    width = (BLOCKS + 1) * 128
    smem = pl.BlockSpec(memory_space=pltpu.SMEM)
    out = pl.pallas_call(
        functools.partial(kernel, nf, ns, nz),
        out_shape=jax.ShapeDtypeStruct((SRCS, CH, 2 * 128), F32),
        in_specs=[smem, smem, smem, pl.BlockSpec(memory_space=pl.ANY)],
        out_specs=pl.BlockSpec(memory_space=pltpu.VMEM),
        scratch_shapes=[
            pltpu.VMEM((CH, SAMPLES), F32),
            pltpu.VMEM((2, 16, SAMPLES), F32),
            pltpu.VMEM((PIECES, 8, 128), F32),
            pltpu.VMEM((nq, own, 8, 128), F32),
            pltpu.VMEM((own, 8, 128), F32),
            pltpu.VMEM((nz, own, 8, 128), F32),
            pltpu.VMEM((PIECES, 8, 128), F32),
            pltpu.VMEM((384, 256), BF16),
            pltpu.VMEM((256, 384), BF16),
            pltpu.VMEM((CH, 192), BF16),
            pltpu.VMEM((BLOCKS * CH, 128), F32),
            pltpu.VMEM((BLOCKS * SROWS, 128), F32),
            pltpu.VMEM((COARSE * CH, width + 128), BF16),
            pltpu.VMEM((256, width), BF16),
            pltpu.SemaphoreType.DMA,
            pltpu.SemaphoreType.DMA((6,)),
            pltpu.SemaphoreType.DMA((4,)),
        ],
        compiler_params=pltpu.CompilerParams(collective_id=0, has_side_effects=True),
    )(fir_taps, space_taps, sources, strain)
    return out.reshape(3, 4, CH, 256)


def solution(mesh):
    nf, ns = mesh.shape["fibre"], mesh.shape["seg"]
    nz = 8 if nf % 8 == 0 else 2
    return jax.shard_map(
        functools.partial(local, nf, ns, nz),
        mesh=mesh,
        in_specs=(P(("fibre", "seg"), None), P(), P(), P()),
        out_specs=P(None, None, ("fibre", "seg"), None),
        check_vma=False,
    )
```

profile of v0, /device:TPU:1, one launch (start us, length us, event | category | flops | bytes accessed | tf_op | source)
XLA Modules:
  0.0 30.8 jit_solution(6858393683485321185)
XLA Ops:
  0.0 29.1 %shard_map.46 = f32[12,24,256]{2,1,0:T(8,128)} custom-call(f32[64]{0:T(128)} %fir_ref.1, f32[31]{0:T(128)} %space_ref.1, s32[3,4]{1,0:T(4,128)} %src_ref.1, f32[24,2048]{1,0:T(8,128)} %strain_ref.1), custom_call_target="tpu_custom_call" | custom-call | tf_op jit(solution)/shard_map/pallas_call | solution.py:340
  29.1 1.7 %copy.6 = f32[3,4,24,256]{3,2,1,0:T(8,128)} copy(f32[3,4,24,256]{3,2,1,0:T(8,128)} %bitcast.1) | data formatting | bytes 589824
where the time goes:
time: 30.9 us; the launch traced here: 30.8 us
  Pallas kernels  29.1 us (94%)
  local copies, waits for them, and re-layouts  1.69 us (5%)
    pallas_call x1, Pallas kernels, local(): pl.pallas_call(functools.partial(kernel, nf, ns, nz), out_shape=jax.Shape...  29.1 us
    unnamed x1, local copies, waits for them, and re-layouts  1.69 us

commit v1 on v0

--- a/solution.py
+++ b/solution.py
@@ -127,51 +127,81 @@
     return smooth / (level + 1e-5)
 
 
+def ring(step, size):
+    return min(step % size, -step % size)
+
+
+def plane_steps(nx):
+    steps = [(dy, dx, dc) for dy in range(4) for dx in range(nx) for dc in range(2)][1:]
+    return sorted(steps, key=lambda s: (-ring(s[0], 4) - ring(s[1], nx), s[2]))
+
+
+def z_steps(nz):
+    return sorted(range(1, nz), key=lambda s: -ring(s, nz))
+
+
 def kernel(
     nf, ns, nz,
-    fir_ref, space_ref, src_ref, strain_ref, out_ref,
+    fir_hbm, space_hbm, src_hbm, strain_ref, out_ref,
+    fir_ref, space_ref, src_ref,
     x_ref, halo_ref, send1, recv1, send2, recv2, gathered,
     fir_w, win_w, own_w, n_ref, s_ref, q_ref, a_ref,
     load_sem, sems, halo_sems,
 ):
     nq = (nf // nz) * ns
+    nx = nf // nz // 2
     own = PIECES // nq
     f, g = lax.axis_index("fibre"), lax.axis_index("seg")
-    plane = lax.div(f, nz) * ns + g
-    z = lax.rem(f, nz)
+    z, row = lax.rem(f, nz), lax.div(f, nz)
+    x, core = lax.rem(row, nx), lax.rem(g, 2)
+    y = lax.div(g, 2) * 2 + lax.div(row, nx)
     line = f * ns + g
     count = nf * ns
 
+    ys = [lax.rem(y + step, 4) for step in range(4)]
+    xs = [lax.rem(x + step, nx) for step in range(nx)]
+    cores = [core, 1 - core]
+    y_fibre = [lax.rem(v, 2) * (nx * nz) + z for v in ys]
+    y_seg = [lax.div(v, 2) * 2 for v in ys]
+    plane_list = plane_steps(nx)
+    z_list = z_steps(nz)
+
     def in_plane(step):
-        other = lax.rem(plane + step, nq)
-        return (lax.div(other, ns) * nz + z, lax.rem(other, ns)), other
+        dy, dx, dc = step
+        return (y_fibre[dy] + xs[dx] * nz, y_seg[dy] + cores[dc])
+
+    def place(step):
+        dy, dx, dc = step
+        return (ys[dy] * nx + xs[dx]) * 2 + cores[dc]
+
+    plane = place((0, 0, 0))
 
     def along_z(step):
-        return (lax.div(f, nz) * nz + lax.rem(z + step, nz), g)
+        return (f - z + lax.rem(z + step, nz), g)
 
     def on_line(step):
         other = lax.rem(line + step + count, count)
         return (lax.div(other, ns), lax.rem(other, ns))
 
-    load = pltpu.make_async_copy(strain_ref, x_ref, load_sem)
-    load.start()
+    loads = [
+        pltpu.make_async_copy(src, dst, load_sem.at[i])
+        for i, (src, dst) in enumerate(
+            [(strain_ref, x_ref), (space_hbm, space_ref), (src_hbm, src_ref), (fir_hbm, fir_ref)]
+        )
+    ]
+    for load in loads:
+        load.start()
+    barrier = pltpu.get_barrier_semaphore()
+    partners = [in_plane(s) for s in plane_list] + [along_z(s) for s in z_list]
+    for device in partners + [on_line(-1), on_line(1)]:
+        pl.semaphore_signal(barrier, inc=1, device_id=device, device_id_type=MESH)
     gathered[...] = jnp.zeros_like(gathered)
-    barrier = pltpu.get_barrier_semaphore()
-
-    @pl.loop(1, nq)
-    def _(step):
-        pl.semaphore_signal(barrier, inc=1, device_id=in_plane(step)[0], device_id_type=MESH)
-
-    @pl.loop(1, nz)
-    def _(step):
-        pl.semaphore_signal(barrier, inc=1, device_id=along_z(step), device_id_type=MESH)
-
-    for step in (-1, 1):
-        pl.semaphore_signal(barrier, inc=1, device_id=on_line(step), device_id_type=MESH)
 
     first_channel = line * CH
+    loads[1].wait()
+    loads[2].wait()
     source_w = source_weights(src_ref, space_ref, first_channel)
-    load.wait()
+    loads[0].wait()
     pad = jnp.zeros((8, SAMPLES), F32)
     high, low = split(jnp.concatenate([x_ref[...], pad], axis=0))
     part = dot(source_w, jnp.concatenate([high, high, low], axis=0))
@@ -181,19 +211,18 @@
 
     pl.semaphore_wait(barrier, nq - 1 + nz - 1 + 2)
 
-    def plane_copy(step):
-        device, other = in_plane(step)
+    def plane_copy(slot, step):
         return pltpu.make_async_remote_copy(
-            src_ref=send1.at[pl.ds(other * own, own), pl.ds(0, 6)],
-            dst_ref=recv1.at[step, :, pl.ds(0, 6)],
+            src_ref=send1.at[pl.ds(place(step) * own, own), pl.ds(0, 6)],
+            dst_ref=recv1.at[slot, :, pl.ds(0, 6)],
             send_sem=sems.at[0], recv_sem=sems.at[1],
-            device_id=device, device_id_type=MESH,
+            device_id=in_plane(step), device_id_type=MESH,
         )
 
-    def z_copy(step):
+    def z_copy(slot, step):
         return pltpu.make_async_remote_copy(
             src_ref=send2.at[:, pl.ds(0, 6)],
-            dst_ref=recv2.at[step, :, pl.ds(0, 6)],
+            dst_ref=recv2.at[slot, :, pl.ds(0, 6)],
             send_sem=sems.at[2], recv_sem=sems.at[3],
             device_id=along_z(step), device_id_type=MESH,
         )
@@ -203,7 +232,7 @@
         return pltpu.make_async_remote_copy(
             src_ref=mine, dst_ref=mine,
             send_sem=sems.at[4], recv_sem=sems.at[5],
-            device_id=in_plane(step)[0], device_id_type=MESH,
+            device_id=in_plane(step), device_id_type=MESH,
         )
 
     def bulk(ref, first, device):
@@ -224,39 +253,38 @@
         device_id=on_line(-1), device_id_type=MESH,
     )
 
-    @pl.loop(1, nq)
-    def _(step):
-        plane_copy(step).start()
-
+    for slot, step in enumerate(plane_list):
+        plane_copy(slot, step).start()
+
+    loads[3].wait()
     fir_w[...] = fir_weights(fir_ref)
     win_w[...] = window_weights()
     own_w[...] = own_weights(space_ref, first_channel, count * CH)
     a_ref[SRCS * FINE :, :] = jnp.zeros((256 - SRCS * FINE, a_ref.shape[1]), BF16)
 
-    all_plane = bulk(recv1.at[pl.ds(1, nq - 1), :, pl.ds(0, 6)], 0, in_plane(1)[0])
-    all_z = bulk(recv2.at[pl.ds(1, nz - 1), :, pl.ds(0, 6)], 2, along_z(1))
-    all_gather = bulk(gathered.at[pl.ds(0, (nq - 1) * own), pl.ds(0, 6)], 4, in_plane(1)[0])
+    peer = in_plane(plane_list[0])
+    all_plane = bulk(recv1.at[:, :, pl.ds(0, 6)], 0, peer)
+    all_z = bulk(recv2.at[:, :, pl.ds(0, 6)], 2, along_z(1))
+    all_gather = bulk(gathered.at[pl.ds(0, (nq - 1) * own), pl.ds(0, 6)], 4, peer)
 
     all_plane.wait_recv()
     total = send1[pl.ds(plane * own, own), 0:6, :]
-    for step in range(1, nq):
-        total = total + recv1[step, :, 0:6, :]
+    for slot in range(nq - 1):
+        total = total + recv1[slot, :, 0:6, :]
     send2[:, 0:6, :] = total
 
-    @pl.loop(1, nz)
-    def _(step):
-        z_copy(step).start()
+    for slot, step in enumerate(z_list):
+        z_copy(slot, step).start()
 
     up.start()
     down.start()
 
     all_z.wait_recv()
-    for step in range(1, nz):
-        total = total + recv2[step, :, 0:6, :]
+    for slot in range(nz - 1):
+        total = total + recv2[slot, :, 0:6, :]
     gathered[pl.ds(plane * own, own), 0:6, :] = total
 
-    @pl.loop(1, nq)
-    def _(step):
+    for step in plane_list:
         gather_copy(step).start()
 
     up.wait_recv()
@@ -332,23 +360,33 @@
     down.wait_send()
 
 
+def copy_out(in_ref, out_ref, sem):
+    copy = pltpu.make_async_copy(in_ref, out_ref, sem)
+    copy.start()
+    copy.wait()
+
+
 def local(nf, ns, nz, strain, fir_taps, space_taps, sources):
     nq = (nf // nz) * ns
     own = PIECES // nq
     width = (BLOCKS + 1) * 128
-    smem = pl.BlockSpec(memory_space=pltpu.SMEM)
+    hbm = pl.BlockSpec(memory_space=pltpu.HBM)
+    result = jax.ShapeDtypeStruct((SRCS, CH, 2 * 128), F32)
     out = pl.pallas_call(
         functools.partial(kernel, nf, ns, nz),
-        out_shape=jax.ShapeDtypeStruct((SRCS, CH, 2 * 128), F32),
-        in_specs=[smem, smem, smem, pl.BlockSpec(memory_space=pl.ANY)],
+        out_shape=result,
+        in_specs=[hbm] * 4,
         out_specs=pl.BlockSpec(memory_space=pltpu.VMEM),
         scratch_shapes=[
+            pltpu.SMEM((TAPS,), F32),
+            pltpu.SMEM((SPACE,), F32),
+            pltpu.SMEM((3, 4), jnp.int32),
             pltpu.VMEM((CH, SAMPLES), F32),
             pltpu.VMEM((2, 16, SAMPLES), F32),
             pltpu.VMEM((PIECES, 8, 128), F32),
-            pltpu.VMEM((nq, own, 8, 128), F32),
+            pltpu.VMEM((nq - 1, own, 8, 128), F32),
             pltpu.VMEM((own, 8, 128), F32),
-            pltpu.VMEM((nz, own, 8, 128), F32),
+            pltpu.VMEM((nz - 1, own, 8, 128), F32),
             pltpu.VMEM((PIECES, 8, 128), F32),
             pltpu.VMEM((384, 256), BF16),
             pltpu.VMEM((256, 384), BF16),
@@ -357,12 +395,22 @@
             pltpu.VMEM((BLOCKS * SROWS, 128), F32),
             pltpu.VMEM((COARSE * CH, width + 128), BF16),
             pltpu.VMEM((256, width), BF16),
-            pltpu.SemaphoreType.DMA,
+            pltpu.SemaphoreType.DMA((4,)),
             pltpu.SemaphoreType.DMA((6,)),
             pltpu.SemaphoreType.DMA((4,)),
         ],
-        compiler_params=pltpu.CompilerParams(collective_id=0, has_side_effects=True),
-    )(fir_taps, space_taps, sources, strain)
+        compiler_params=pltpu.CompilerParams(
+            collective_id=0, has_side_effects=True, vmem_limit_bytes=16 << 20
+        ),
+    )(*[pltpu.with_memory_space_constraint(v, pltpu.HBM) for v in (fir_taps, space_taps, sources, strain)])
+    out = pl.pallas_call(
+        copy_out,
+        out_shape=result,
+        in_specs=[pl.BlockSpec(memory_space=pltpu.VMEM)],
+        out_specs=pl.BlockSpec(memory_space=pltpu.HBM),
+        scratch_shapes=[pltpu.SemaphoreType.DMA],
+        compiler_params=pltpu.CompilerParams(vmem_limit_bytes=16 << 20),
+    )(out)
     return out.reshape(3, 4, CH, 256)
 
 

time: 30.9 us -> 27.3 us (0.88)
  Pallas kernels: 29.1 us -> 27.2 us
  local copies, waits for them, and re-layouts: 1.69 us -> 0 us
    pallas_call x1 -> x2, Pallas kernels: 29.1 us -> 27.2 us  [the longest x1 26.5 us: local(): pl.pallas_call(functools.partial(kernel, nf, ns, nz), out_shape=result, i...]
    unnamed x1 -> x0, local copies, waits for them, and re-layouts: 1.69 us -> none
where the time goes in v1:
time: 27.3 us; the launch traced here: 27.2 us
  Pallas kernels  27.2 us (100%)
    pallas_call x1, Pallas kernels, local(): pl.pallas_call(functools.partial(kernel, nf, ns, nz), out_shape=result, i...  26.5 us
    pallas_call x1, Pallas kernels, local(): pl.pallas_call(copy_out, out_shape=result, in_specs=[pl.BlockSpec(memory_...  0.72 us

profile of v1, /device:TPU:1, one launch (start us, length us, event | category | flops | bytes accessed | tf_op | source)
XLA Modules:
  0.0 27.2 jit_solution(13457504969055830462)
XLA Ops:
  0.0 26.5 %shard_map.46.in_ref = f32[12,24,256]{2,1,0:T(8,128)S(1)} custom-call(f32[64]{0:T(128)} %fir_hbm.1, f32[31]{0:T(128)} %space_hbm.1, s32[3,4]{1,0:T(4,128)} %src_hbm.1, f32[24,2048]{1,0:T(8,128)} %strain_ref.1), custom_call_target="tpu_custom_call" | custom-call | tf_op jit(solution)/shard_map/pallas_call | solution.py:375
  26.5 0.7 %shard_map.47 = f32[12,24,256]{2,1,0:T(8,128)} custom-call(f32[12,24,256]{2,1,0:T(8,128)S(1)} %shard_map.46.in_ref), custom_call_target="tpu_custom_call" | custom-call | tf_op jit(solution)/shard_map/pallas_call | solution.py:406

commit v2 on v1

--- a/solution.py
+++ b/solution.py
@@ -22,11 +22,7 @@
 SROWS = 16
 FINE = 16
 COARSE = 8
-PIECES = 32
-
-
-def source_row(i):
-    return i if i < 6 else i + 2
+PIECES = 24
 
 
 def dot(a, b, contract=((1,), (0,))):
@@ -53,7 +49,8 @@
     row, lane = iota(shape, 0), iota(shape, 1)
     chosen = jnp.full(shape, -(1 << 20), jnp.int32)
     for i in range(SRCS):
-        chosen = jnp.where(row == source_row(i), src_ref[i // 4, i % 4], chosen)
+        here = (row == i) if i < 8 else (row == i) | (row == i + 4)
+        chosen = jnp.where(here, src_ref[i // 4, i % 4], chosen)
     part, r = lane // 32, lane % 32
     tap = jnp.where(r < CH, first + r - chosen + HALF, -1)
     w = jnp.zeros(shape, F32)
@@ -136,6 +133,17 @@
     return sorted(steps, key=lambda s: (-ring(s[0], 4) - ring(s[1], nx), s[2]))
 
 
+def owner(y, x, nx):
+    return lax.div(y, 2) * lax.div(x, 2) if nx > 1 else lax.div(y, 3)
+
+
+def owner_chip(y, x, nx):
+    if nx == 1:
+        return y
+    half = lax.div(y, 2)
+    return (1 - half) * (nx * y + x) + half * (2 * nx + 2 * (y - 2) + x)
+
+
 def z_steps(nz):
     return sorted(range(1, nz), key=lambda s: -ring(s, nz))
 
@@ -150,7 +158,8 @@
 ):
     nq = (nf // nz) * ns
     nx = nf // nz // 2
-    own = PIECES // nq
+    owners = nq * 3 // 4
+    own = PIECES // owners
     f, g = lax.axis_index("fibre"), lax.axis_index("seg")
     z, row = lax.rem(f, nz), lax.div(f, nz)
     x, core = lax.rem(row, nx), lax.rem(g, 2)
@@ -170,11 +179,13 @@
         dy, dx, dc = step
         return (y_fibre[dy] + xs[dx] * nz, y_seg[dy] + cores[dc])
 
-    def place(step):
+    is_owner = owner(y, x, nx) == 0
+
+    def piece(step):
         dy, dx, dc = step
-        return (ys[dy] * nx + xs[dx]) * 2 + cores[dc]
-
-    plane = place((0, 0, 0))
+        return owner_chip(ys[dy], xs[dx], nx) * 2 + cores[dc]
+
+    mine = piece((0, 0, 0))
 
     def along_z(step):
         return (f - z + lax.rem(z + step, nz), g)
@@ -192,10 +203,16 @@
     for load in loads:
         load.start()
     barrier = pltpu.get_barrier_semaphore()
-    partners = [in_plane(s) for s in plane_list] + [along_z(s) for s in z_list]
-    for device in partners + [on_line(-1), on_line(1)]:
-        pl.semaphore_signal(barrier, inc=1, device_id=device, device_id_type=MESH)
-    gathered[...] = jnp.zeros_like(gathered)
+
+    def greet(devices):
+        for device in devices:
+            pl.semaphore_signal(barrier, inc=1, device_id=device, device_id_type=MESH)
+
+    @pl.when(is_owner)
+    def _():
+        greet([in_plane(s) for s in plane_list] + [along_z(s) for s in z_list])
+
+    greet([on_line(-1), on_line(1)])
 
     first_channel = line * CH
     loads[1].wait()
@@ -205,32 +222,37 @@
     pad = jnp.zeros((8, SAMPLES), F32)
     high, low = split(jnp.concatenate([x_ref[...], pad], axis=0))
     part = dot(source_w, jnp.concatenate([high, high, low], axis=0))
+    upper = iota((8, 128), 0) < 4
     for b in range(BLOCKS):
-        for h in range(2):
-            send1[2 * b + h] = part[8 * h : 8 * h + 8, 128 * b : 128 * b + 128]
-
-    pl.semaphore_wait(barrier, nq - 1 + nz - 1 + 2)
+        send1[b] = part[:8, 128 * b : 128 * b + 128]
+    for b in range(0, BLOCKS, 2):
+        send1[BLOCKS + b // 2] = jnp.where(
+            upper, part[8:, 128 * b : 128 * b + 128], part[8:, 128 * b + 128 : 128 * b + 256]
+        )
+
+    pl.when(is_owner)(lambda: pl.semaphore_wait(barrier, owners - 1 + nz - 1 + 2))
+    pl.when(~is_owner)(lambda: pl.semaphore_wait(barrier, owners + 2))
 
     def plane_copy(slot, step):
         return pltpu.make_async_remote_copy(
-            src_ref=send1.at[pl.ds(place(step) * own, own), pl.ds(0, 6)],
-            dst_ref=recv1.at[slot, :, pl.ds(0, 6)],
+            src_ref=send1.at[pl.ds(piece(step) * own, own)],
+            dst_ref=recv1.at[slot],
             send_sem=sems.at[0], recv_sem=sems.at[1],
             device_id=in_plane(step), device_id_type=MESH,
         )
 
     def z_copy(slot, step):
         return pltpu.make_async_remote_copy(
-            src_ref=send2.at[:, pl.ds(0, 6)],
-            dst_ref=recv2.at[slot, :, pl.ds(0, 6)],
+            src_ref=send2,
+            dst_ref=recv2.at[slot],
             send_sem=sems.at[2], recv_sem=sems.at[3],
             device_id=along_z(step), device_id_type=MESH,
         )
 
     def gather_copy(step):
-        mine = gathered.at[pl.ds(plane * own, own), pl.ds(0, 6)]
+        pieces = gathered.at[pl.ds(mine * own, own)]
         return pltpu.make_async_remote_copy(
-            src_ref=mine, dst_ref=mine,
+            src_ref=pieces, dst_ref=pieces,
             send_sem=sems.at[4], recv_sem=sems.at[5],
             device_id=in_plane(step), device_id_type=MESH,
         )
@@ -254,7 +276,8 @@
     )
 
     for slot, step in enumerate(plane_list):
-        plane_copy(slot, step).start()
+        to_owner = owner(ys[step[0]], xs[step[1]], nx) == 0
+        pl.when(to_owner)(plane_copy(slot, step).start)
 
     loads[3].wait()
     fir_w[...] = fir_weights(fir_ref)
@@ -263,29 +286,39 @@
     a_ref[SRCS * FINE :, :] = jnp.zeros((256 - SRCS * FINE, a_ref.shape[1]), BF16)
 
     peer = in_plane(plane_list[0])
-    all_plane = bulk(recv1.at[:, :, pl.ds(0, 6)], 0, peer)
-    all_z = bulk(recv2.at[:, :, pl.ds(0, 6)], 2, along_z(1))
-    all_gather = bulk(gathered.at[pl.ds(0, (nq - 1) * own), pl.ds(0, 6)], 4, peer)
-
-    all_plane.wait_recv()
-    total = send1[pl.ds(plane * own, own), 0:6, :]
-    for slot in range(nq - 1):
-        total = total + recv1[slot, :, 0:6, :]
-    send2[:, 0:6, :] = total
-
-    for slot, step in enumerate(z_list):
-        z_copy(slot, step).start()
+    all_plane = bulk(recv1, 0, peer)
+    all_z = bulk(recv2, 2, along_z(1))
+
+    def some_sent(n):
+        return bulk(send1.at[pl.ds(0, n * own)], 0, peer)
+
+    def some_gathered(n):
+        return bulk(gathered.at[pl.ds(0, n * own)], 4, peer)
+
+    all_sent = bulk(recv1, 4, peer)
+
+    @pl.when(is_owner)
+    def _():
+        all_plane.wait_recv()
+        total = send1[pl.ds(mine * own, own)]
+        for slot in range(nq - 1):
+            total = total + recv1[slot]
+        send2[...] = total
+        for slot, step in enumerate(z_list):
+            z_copy(slot, step).start()
 
     up.start()
     down.start()
 
-    all_z.wait_recv()
-    for slot in range(nz - 1):
-        total = total + recv2[slot, :, 0:6, :]
-    gathered[pl.ds(plane * own, own), 0:6, :] = total
-
-    for step in plane_list:
-        gather_copy(step).start()
+    @pl.when(is_owner)
+    def _():
+        all_z.wait_recv()
+        total = send2[...]
+        for slot in range(nz - 1):
+            total = total + recv2[slot]
+        gathered[pl.ds(mine * own, own)] = total
+        for step in plane_list:
+            gather_copy(step).start()
 
     up.wait_recv()
     down.wait_recv()
@@ -313,15 +346,20 @@
         q_ref[:, (b + 1) * 128 : (b + 2) * 128] = jnp.concatenate(shifted, axis=0).astype(BF16)
         here = following
 
-    all_gather.wait_recv()
-    records = gathered[...].reshape(BLOCKS * SROWS, 128)
+    pl.when(is_owner)(lambda: some_gathered(owners - 1).wait_recv())
+    pl.when(~is_owner)(lambda: some_gathered(owners).wait_recv())
+    pieces = []
+    for b in range(BLOCKS):
+        rest = gathered[BLOCKS + b // 2]
+        pieces += [gathered[b], pltpu.roll(rest, 4, 0) if b % 2 else rest]
+    records = jnp.concatenate(pieces, axis=0)
     s_ref[...] = normalized(records, SROWS, fir_w[...], win_w[...])
     shift, lane = iota((FINE, 128), 0), iota((FINE, 128), 1)
     for i in range(SRCS):
         before = jnp.zeros((FINE, 128), F32)
         for b in range(BLOCKS + 1):
             if b < BLOCKS:
-                row = b * SROWS + source_row(i)
+                row = b * SROWS + i
                 wide = jnp.broadcast_to(s_ref[row : row + 1, :], (FINE, 128))
                 here = pltpu.roll(wide, 0, 1, stride=1, stride_axis=0)
             else:
@@ -353,9 +391,13 @@
                 if COARSE * tile + k < SRCS:
                     out_ref[COARSE * tile + k, :, 128 * half : 128 * half + 128] = v[k]
 
-    all_plane.wait_send()
-    all_z.wait_send()
-    all_gather.wait_send()
+    @pl.when(is_owner)
+    def _():
+        some_sent(owners - 1).wait_send()
+        all_z.wait_send()
+        all_sent.wait_send()
+
+    pl.when(~is_owner)(lambda: some_sent(owners).wait_send())
     up.wait_send()
     down.wait_send()
 
@@ -368,7 +410,7 @@
 
 def local(nf, ns, nz, strain, fir_taps, space_taps, sources):
     nq = (nf // nz) * ns
-    own = PIECES // nq
+    own = PIECES // (nq * 3 // 4)
     width = (BLOCKS + 1) * 128
     hbm = pl.BlockSpec(memory_space=pltpu.HBM)
     result = jax.ShapeDtypeStruct((SRCS, CH, 2 * 128), F32)

time: 27.3 us -> 26.9 us (0.985)
  Pallas kernels: 27.2 us -> 26.8 us
    pallas_call x1, Pallas kernels: 26.5 us -> 26.1 us  [local(): pl.pallas_call(functools.partial(kernel, nf, ns, nz), out_shape=result, i...]
where the time goes in v2:
time: 26.9 us; the launch traced here: 26.8 us
  Pallas kernels  26.8 us (100%)
    pallas_call x1, Pallas kernels, local(): pl.pallas_call(functools.partial(kernel, nf, ns, nz), out_shape=result, i...  26.1 us
    pallas_call x1, Pallas kernels, local(): pl.pallas_call(copy_out, out_shape=result, in_specs=[pl.BlockSpec(memory_...  0.72 us

profile of v2, /device:TPU:1, one launch (start us, length us, event | category | flops | bytes accessed | tf_op | source)
XLA Modules:
  0.0 26.8 jit_solution(14870031431249507489)
XLA Ops:
  0.0 26.1 %shard_map.46.in_ref = f32[12,24,256]{2,1,0:T(8,128)S(1)} custom-call(f32[64]{0:T(128)} %fir_hbm.1, f32[31]{0:T(128)} %space_hbm.1, s32[3,4]{1,0:T(4,128)} %src_hbm.1, f32[24,2048]{1,0:T(8,128)} %strain_ref.1), custom_call_target="tpu_custom_call" | custom-call | tf_op jit(solution)/shard_map/pallas_call | solution.py:417
  26.1 0.7 %shard_map.47 = f32[12,24,256]{2,1,0:T(8,128)} custom-call(f32[12,24,256]{2,1,0:T(8,128)S(1)} %shard_map.46.in_ref), custom_call_target="tpu_custom_call" | custom-call | tf_op jit(solution)/shard_map/pallas_call | solution.py:448
